TPU v7x, 32 devices: a whole 2x2x4 slice. The times are simulated.
32 devices in a mesh: groups: 2 (over y), ctx: 4 (over z), head: 4 (over x, core).
Axes of the slice: x: 2, y: 2, z: 4, core: 2. Of those that a mesh axis runs over, the one named last changes fastest.
Arguments:
- query_rows: bfloat16 [3072, 3072], P(('groups', 'ctx', 'head')), parts along dimension 0, may hold values from -150 to 150
- key_rows: bfloat16 [3072, 3072], P(('groups', 'ctx', 'head')), parts along dimension 0, may hold values from -6 to 6
- value_rows: bfloat16 [3072, 3072], P(('groups', 'ctx', 'head')), parts along dimension 0, may hold values from -6 to 6
- tile_mask: int32 [8, 27], P(('groups', 'ctx')), parts along dimension 0, may hold values from 0 to 1, as said below
Outputs:
- attended: bfloat16 [3072, 3072], P(('groups', 'ctx', 'head')), parts along dimension 0
There are 2 independent parts, one for each index of `groups`. A program takes and returns all parts, laid end to end along the dimension named above; each array names one. Nothing has to cross between parts.
Inputs may be any that keep to these rules, and one draw needn't show every extreme that they name: `tile_mask`: entry o of row i is 1 only where the key tile of offset o lies inside the grid; entry 13 is always 1; a row has at most 4 ones, and some row has exactly 4.
All inputs are finite; a program needn't handle non-finite values.
Results may differ from a plain program's by a relative error of at most 0.0023.
Values may be sent and summed in bfloat16 or wider, within the bound.
No kernel may reach another device: no remote copies, remote signals or barrier semaphores. Data moves between devices by JAX's collectives and lax.ppermute only.
A program may use at most 64 MiB of HBM per device.

v0:
```python
import math
import jax
import jax.numpy as jnp
from jax import lax
from jax.sharding import PartitionSpec as P

HDIM = 128


def passed_along(block, axis, distance):
    devices = range(lax.axis_size(axis))
    route = [((i - distance) % len(devices), i) for i in devices]
    return lax.ppermute(block, axis, route)


def on_device(query_rows, key_rows, value_rows, tile_mask):
    cycle_size = lax.axis_size("ctx")
    grid_rows = max(2, cycle_size // 8)
    grid_cols = cycle_size // grid_rows
    query_local, key_local, value_local = (
        lax.all_to_all(query_rows, "head", split_axis=1, concat_axis=0, tiled=True),
        lax.all_to_all(key_rows, "head", split_axis=1, concat_axis=0, tiled=True),
        lax.all_to_all(value_rows, "head", split_axis=1, concat_axis=0, tiled=True),
    )
    feature_width = query_local.shape[1]
    head_count = feature_width // HDIM
    frames = tile_mask.shape[0]
    tile_len = query_local.shape[0] // frames
    key_value = jnp.stack([key_local, value_local]).reshape(2, frames, tile_len, feature_width)
    row_parts = [passed_along(key_value, "ctx", shift_by) for shift_by in (1, -1)]
    row_strip = jnp.stack([row_parts[0], key_value, row_parts[1]])
    column_parts = [
        passed_along(row_strip, "ctx", shift_by) for shift_by in (grid_cols, -grid_cols)
    ]
    window = jnp.stack([column_parts[0], row_strip, column_parts[1]])
    key_tiles = window[:, :, 0].reshape(9 * frames, tile_len, feature_width)
    value_tiles = window[:, :, 1].reshape(9 * frames, tile_len, feature_width)
    kept_mask = tile_mask == 1
    first_offset = 9
    slot_count = 9
    slot_order = jnp.arange(first_offset, first_offset + slot_count, dtype=jnp.int32)[None, :]
    slot_kept = kept_mask[:, first_offset : first_offset + slot_count]
    frame_ids = jnp.arange(frames, dtype=jnp.int32)[:, None]
    source_frame = jnp.clip(frame_ids + slot_order // 9 - 1, 0, frames - 1)
    source = slot_order % 9 * frames + source_frame
    kept_cols = jnp.repeat(slot_kept, tile_len, axis=1)[:, None, :]
    score_scale = 1.0 / math.sqrt(HDIM)

    def one_head(head_index):
        column_start = head_index * HDIM
        key_head = lax.dynamic_slice_in_dim(key_tiles, column_start, HDIM, 2)
        value_head = lax.dynamic_slice_in_dim(value_tiles, column_start, HDIM, 2)
        query_head = lax.dynamic_slice_in_dim(query_local, column_start, HDIM, 1).reshape(
            frames, tile_len, HDIM
        )
        picked_keys = jnp.take(key_head, source, axis=0).reshape(
            frames, slot_count * tile_len, HDIM
        )
        picked_values = jnp.take(value_head, source, axis=0).reshape(
            frames, slot_count * tile_len, HDIM
        )
        scores = (
            jnp.einsum("fqd,fkd->fqk", query_head, picked_keys, preferred_element_type=jnp.float32)
            * score_scale
        )
        row_peak = jnp.max(jnp.where(kept_cols, scores, -jnp.inf), axis=2, keepdims=True)
        weight = jnp.exp(jnp.where(kept_cols, scores - row_peak, -jnp.inf))
        row_total = jnp.sum(weight, axis=2, keepdims=True)
        rounded = weight.astype(jnp.bfloat16)
        mixed = jnp.einsum(
            "fqk,fkd->fqd", rounded, picked_values, preferred_element_type=jnp.float32
        )
        return (mixed / row_total).astype(jnp.bfloat16)

    result = lax.map(one_head, jnp.arange(head_count, dtype=jnp.int32))
    result = jnp.transpose(result, (1, 2, 0, 3)).reshape(frames * tile_len, feature_width)
    return lax.all_to_all(result, "head", split_axis=0, concat_axis=1, tiled=True)


def solution(mesh):
    placed = (
        P(("groups", "ctx", "head"), None),
        P(("groups", "ctx", "head"), None),
        P(("groups", "ctx", "head"), None),
        P(("groups", "ctx"), None),
    )
    return jax.shard_map(
        on_device,
        mesh=mesh,
        in_specs=placed,
        out_specs=P(("groups", "ctx", "head"), None),
        check_vma=False,
    )
```

profile of v0, /device:TPU:0, one launch (start us, length us, event | category | flops | bytes accessed | tf_op | source)
XLA Modules:
  0.0 327.5 jit_solution(2252575000279086143)
XLA Ops:
  0.0 1.9 copy.44
  1.9 4.2 %all-to-all-start.1 = ((bf16[96,4,768]{2,0,1:T(8,128)(2,1)}), bf16[96,4,768]{2,0,1:T(8,128)(2,1)S(1)}, u32[]{:S(2)}, u32[]{:S(2)}) async-start(bf16[96,4,768]{2,0,1:T(8,128)(2,1)} %bitcast.57), calls=%async_computation.1 | async-start | bytes 1179648 | tf_op jit(solution)/shard_map/all_to_all | solution.py:22
  7.3 8.4 %all-to-all-done.1 = bf16[96,4,768]{2,0,1:T(8,128)(2,1)S(1)} async-done(((bf16[96,4,768]{2,0,1:T(8,128)(2,1)}), bf16[96,4,768]{2,0,1:T(8,128)(2,1)S(1)}, u32[]{:S(2)}, u32[]{:S(2)}) %all-to-all-start.1) | async-done | bytes 589856 | tf_op jit(solution)/shard_map/all_to_all | solution.py:22
  15.7 11.9 %all_to_all.70 = bf16[96,4,768]{2,0,1:T(8,128)(2,1)S(1)} all-to-all(bf16[96,4,768]{2,0,1:T(8,128)(2,1)S(1)} %bitcast.84), channel_id=1, replica_groups=mesh['groups'=2,'ctx'=4,'head'=4] {'head'}, dimensions={1} | all-to-all | bytes 1179648 | tf_op jit(solution)/shard_map/all_to_all | solution.py:23
  27.7 2.3 collective-permute-start
  30.0 2.1 collective-permute-start.1
  32.1 26.8 %collective-permute-done = bf16[2,1,384,768]{3,2,0,1:T(8,128)(2,1)S(1)} collective-permute-done((bf16[2,1,384,768]{3,2,0,1:T(8,128)(2,1)S(1)}, bf16[2,1,384,768]{3,2,0,1:T(8,128)(2,1)S(1)}, u32[]{:S(2)}, u32[]{:S(2)}) %collective-permute-start) | collective-permute-done | bytes 1179680 | tf_op jit(solution)/shard_map/ppermute | solution.py:13
  58.9 23.7 %collective-permute-done.1 = bf16[2,1,384,768]{3,2,0,1:T(8,128)(2,1)S(1)} collective-permute-done((bf16[2,1,384,768]{3,2,0,1:T(8,128)(2,1)S(1)}, bf16[2,1,384,768]{3,2,0,1:T(8,128)(2,1)S(1)}, u32[]{:S(2)}, u32[]{:S(2)}) %collective-permute-start.1) | collective-permute-done | bytes 1179680 | tf_op jit(solution)/shard_map/ppermute | solution.py:13
  82.7 2.0 fusion.32
  86.9 4.2 %all-to-all-start = ((bf16[96,4,768]{2,0,1:T(8,128)(2,1)}), bf16[96,4,768]{2,0,1:T(8,128)(2,1)}, u32[]{:S(2)}, u32[]{:S(2)}) async-start(bf16[96,4,768]{2,0,1:T(8,128)(2,1)} %bitcast.83), calls=%async_computation | async-start | bytes 1179648 | tf_op jit(solution)/shard_map/all_to_all | solution.py:21
  91.2 148.5 %collective-permute-done.2 = bf16[3,2,1,384,768]{4,3,1,0,2:T(8,128)(2,1)} collective-permute-done((bf16[3,2,1,384,768]{4,3,1,0,2:T(8,128)(2,1)}, bf16[3,2,1,384,768]{4,3,1,0,2:T(8,128)(2,1)}, u32[]{:S(2)}, u32[]{:S(2)}) %collective-permute-start.2) | collective-permute-done | bytes 3538976 | tf_op jit(solution)/shard_map/ppermute | solution.py:13
  239.6 8.4 %pad_maximum_fusion = bf16[3,3,2,1,384,768]{5,4,2,1,3,0:T(8,128)(2,1)} fusion(bf16[1,3,2,1,384,768]{5,4,2,1,3,0:T(8,128)(2,1)} %bitcast.11, bf16[1,3,2,1,384,768]{5,4,2,1,3,0:T(8,128)(2,1)S(1)} %get-tuple-element.112), kind=kLoop, calls=%fused_computation.36 | loop fusion | flops 10616832 | bytes 17694720 | tf_op jit(solution)/shard_map/stack | solution.py:35
  248.0 8.9 %fusion.36 = (bf16[3,3,1,1,384,768]{5,4,2,1,3,0:T(8,128)(2,1)}, bf16[3,3,1,1,384,768]{5,4,2,1,3,0:T(8,128)(2,1)}) fusion(bf16[3,3,2,1,384,768]{5,4,2,1,3,0:T(8,128)(2,1)} %pad_maximum_fusion), kind=kLoop, calls=%fused_computation.48 | loop fusion | bytes 21233664 | tf_op jit(solution)/shard_map/slice | solution.py:37
  256.9 55.6 %while.12 = (s32[]{:T(128)}, bf16[6,1,384,128]{3,2,1,0:T(8,128)(2,1)}, s32[6]{0:T(128)S(1)}, bf16[384,768]{1,0:T(8,128)(2,1)}, bf16[9,384,768]{2,1,0:T(8,128)(2,...) while((s32[]{:T(128)}, ...), condition=%wide.region_3.5_spmd.clone.clone, body=%wide.region_0.4_spmd.clone.clone.sunk | while | flops 692404736 | bytes 28541528 | solution.py:75
  258.2 1.6 constant_dynamic-slice_fusion.3
  261.6 1.9 select_reduce_fusion.2
  264.6 1.6 fusion.50
  267.5 1.6 constant_dynamic-slice_fusion.3
  270.9 1.9 select_reduce_fusion.2
  273.8 1.6 fusion.50
  276.7 1.6 constant_dynamic-slice_fusion.3
  280.1 1.9 select_reduce_fusion.2
  283.1 1.6 fusion.50
  286.0 1.6 constant_dynamic-slice_fusion.3
  289.4 1.9 select_reduce_fusion.2
  292.4 1.6 fusion.50
  298.7 1.9 select_reduce_fusion.2
  301.6 1.6 fusion.50
  304.5 1.6 constant_dynamic-slice_fusion.3
  307.9 1.9 select_reduce_fusion.2
  310.9 1.6 fusion.50
  314.7 11.9 %all_to_all.71 = bf16[4,96,768]{2,1,0:T(8,128)(2,1)S(1)} all-to-all(bf16[4,96,768]{2,1,0:T(8,128)(2,1)S(1)} %all_to_all.62), channel_id=1, replica_groups=mesh['groups'=2,'ctx'=4,'head'=4] {'head'}, dimensions={0} | all-to-all | bytes 1179648 | tf_op jit(solution)/shard_map/all_to_all | solution.py:77
  (77 shorter events, 29.2 us)
Async XLA Ops:
  1.9 13.8 %all-to-all-start.1 = ((bf16[96,4,768]{2,0,1:T(8,128)(2,1)}), bf16[96,4,768]{2,0,1:T(8,128)(2,1)S(1)}, u32[]{:S(2)}, u32[]{:S(2)}) async-start(bf16[96,4,768]{2,0,1:T(8,128)(2,1)} %bitcast.57), calls=%async_computation.1 | async-start | bytes 1179648 | tf_op jit(solution)/shard_map/all_to_all | solution.py:22
  27.7 31.2 %collective-permute-start = (bf16[2,1,384,768]{3,2,0,1:T(8,128)(2,1)S(1)}, bf16[2,1,384,768]{3,2,0,1:T(8,128)(2,1)S(1)}, u32[]{:S(2)}, u32[]{:S(2)}) collective-permute-start(bf16[2,1,384,768]{3,2,0,1:T(8,128)(2,1)S(1)} %get-tuple-element.115), channel_id=1, source_target_pairs={{12,0},{0,4},{4,8},{8,12},{13,1},{1,5},{5,9},{9,13},{14,2},{2,6},{... | collective-permute-start | bytes 3538952 | tf_op jit(solution)/shard_map/ppermute | solution.py:13
  30.0 52.6 %collective-permute-start.1 = (bf16[2,1,384,768]{3,2,0,1:T(8,128)(2,1)S(1)}, bf16[2,1,384,768]{3,2,0,1:T(8,128)(2,1)S(1)}, u32[]{:S(2)}, u32[]{:S(2)}) collective-permute-start(bf16[2,1,384,768]{3,2,0,1:T(8,128)(2,1)S(1)} %get-tuple-element.115), channel_id=1, source_target_pairs={{4,0},{8,4},{12,8},{0,12},{5,1},{9,5},{13,9},{1,13},{6,2},{10,6},{... | collective-permute-start | bytes 3538952 | tf_op jit(solution)/shard_map/ppermute | solution.py:13
  82.7 3.3 %copy-start = (bf16[96,3072]{1,0:T(8,128)(2,1)S(1)}, bf16[96,3072]{1,0:T(8,128)(2,1)}, u32[]{:S(2)}) copy-start(bf16[96,3072]{1,0:T(8,128)(2,1)} %param.8) | copy-start | bytes 1769476
  82.7 8.4 %copy-start.1 = (s32[1,27]{1,0:T(1,128)S(1)}, s32[1,27]{1,0:T(1,128)}, u32[]{:S(2)}) copy-start(s32[1,27]{1,0:T(1,128)} %param.11) | copy-start | bytes 328
  84.7 154.9 %collective-permute-start.2 = (bf16[3,2,1,384,768]{4,3,1,0,2:T(8,128)(2,1)}, bf16[3,2,1,384,768]{4,3,1,0,2:T(8,128)(2,1)}, u32[]{:S(2)}, u32[]{:S(2)}) collective-permute-start(bf16[3,2,1,384,768]{4,3,1,0,2:T(8,128)(2,1)} %get-tuple-element.113), channel_id=1, source_target_pairs={{8,0},{12,4},{0,8},{4,12},{9,1},{13,5},{1,9},{5,13},{10,2},{14,6},... | collective-permute-start | bytes 10616840 | tf_op jit(solution)/shard_map/ppermute | solution.py:13
  86.9 170.0 %all-to-all-start = ((bf16[96,4,768]{2,0,1:T(8,128)(2,1)}), bf16[96,4,768]{2,0,1:T(8,128)(2,1)}, u32[]{:S(2)}, u32[]{:S(2)}) async-start(bf16[96,4,768]{2,0,1:T(8,128)(2,1)} %bitcast.83), calls=%async_computation | async-start | bytes 1179648 | tf_op jit(solution)/shard_map/all_to_all | solution.py:21
where the time goes:
time: 328 us; the launch traced here: 327 us
  waiting for transfers between devices  207 us (63%)
  local copies, waits for them, and re-layouts  38.3 us (12%)
  blocking collectives  23.8 us (7%)
  matrix products  21.1 us (6%)
  other arithmetic  18.6 us (6%)
  starting transfers between devices  14.1 us (4%)
  loops' own time  4.07 us (1%)
    ppermute x3, waiting for transfers between devices, passed_along(): return lax.ppermute(block, axis, route)  199 us
    all_to_all x1, blocking collectives, on_device(): lax.all_to_all(result, 'head', split_axis=0, concat_axis=1, tiled=True)  11.9 us
    all_to_all x1, blocking collectives, on_device(): lax.all_to_all(value_rows, 'head', split_axis=1, concat_axis=0, tiled=True)  11.9 us
    dot_general x6, matrix products, one_head(): jnp.einsum('fqd,fkd->fqk', query_head, picked_keys, preferred_element_typ...  11.2 us
    another operation x2, other arithmetic, on_device(): window = jnp.stack([column_parts[0], row_strip, column_parts[1]])  10.4 us
    dot_general x6, matrix products, one_head(): jnp.einsum('fqk,fkd->fqd', rounded, picked_values, preferred_element_type...  9.83 us
    dynamic_slice x6, local copies, waits for them, and re-layouts, one_head(): value_head = lax.dynamic_slice_in_dim(value_tiles, column_start, HDIM, 2)  9.42 us
    slice x1, local copies, waits for them, and re-layouts, on_device(): value_tiles = window[:, :, 1].reshape(9 * frames, tile_len, feature_width)  8.9 us
  transfers between devices with their start and end apart: 5, of which 4 were waited for; matrix products, arithmetic and copies ran while one was open for 6% of the time, Pallas kernels for 0%

commit v1 on v0

--- a/solution.py
+++ b/solution.py
@@ -5,6 +5,18 @@
 from jax.sharding import PartitionSpec as P
 
 HDIM = 128
+
+
+def sent_to_each(x, axis, split, join):
+    ways, here = (lax.axis_size(axis), lax.axis_index(axis))
+    width = x.shape[split] // ways
+    turned = jnp.roll(x, -here * width, axis=split)
+    got = [lax.slice_in_dim(turned, 0, width, axis=split)]
+    for far in range(1, ways):
+        sent = lax.slice_in_dim(turned, far * width, (far + 1) * width, axis=split)
+        got.append(lax.ppermute(sent, axis, [(d, (d + far) % ways) for d in range(ways)]))
+    line = jnp.concatenate(got[::-1], axis=join)
+    return jnp.roll(line, (here + 1) * got[0].shape[join], axis=join)
 
 
 def passed_along(block, axis, distance):
@@ -20,7 +32,7 @@
     query_local, key_local, value_local = (
         lax.all_to_all(query_rows, "head", split_axis=1, concat_axis=0, tiled=True),
         lax.all_to_all(key_rows, "head", split_axis=1, concat_axis=0, tiled=True),
-        lax.all_to_all(value_rows, "head", split_axis=1, concat_axis=0, tiled=True),
+        sent_to_each(value_rows, "head", 1, 0),
     )
     feature_width = query_local.shape[1]
     head_count = feature_width // HDIM

time: 328 us -> 320 us (0.976)
  blocking collectives: 23.8 us -> 11.9 us
    all_to_all x1 -> x0, blocking collectives: 11.9 us -> none  [on_device(): lax.all_to_all(value_rows, 'head', split_axis=1, concat_axis=0, tiled=True)]
  transfers between devices with their start and end apart: 5 -> 8, of which waited for: 4 -> 5; matrix products, arithmetic and copies ran while one was open for 6% -> 6% of each run, Pallas kernels for 0% -> 0%
where the time goes in v1:
time: 320 us; the launch traced here: 319 us
  waiting for transfers between devices  208 us (65%)
  local copies, waits for them, and re-layouts  37.6 us (12%)
  matrix products  21 us (7%)
  other arithmetic  20.2 us (6%)
  starting transfers between devices  16.1 us (5%)
  blocking collectives  11.9 us (4%)
  loops' own time  4.4 us (1%)
    ppermute x3, waiting for transfers between devices, passed_along(): return lax.ppermute(block, axis, route)  199 us
    all_to_all x1, blocking collectives, on_device(): lax.all_to_all(result, 'head', split_axis=0, concat_axis=1, tiled=True)  11.9 us
    dot_general x6, matrix products, one_head(): jnp.einsum('fqd,fkd->fqk', query_head, picked_keys, preferred_element_typ...  11.2 us
    another operation x2, other arithmetic, on_device(): window = jnp.stack([column_parts[0], row_strip, column_parts[1]])  10.4 us
    dot_general x6, matrix products, one_head(): jnp.einsum('fqk,fkd->fqd', rounded, picked_values, preferred_element_type...  9.83 us
    dynamic_slice x6, local copies, waits for them, and re-layouts, one_head(): value_head = lax.dynamic_slice_in_dim(value_tiles, column_start, HDIM, 2)  9.44 us
    slice x1, local copies, waits for them, and re-layouts, on_device(): value_tiles = window[:, :, 1].reshape(9 * frames, tile_len, feature_width)  8.9 us
    all_to_all x1, waiting for transfers between devices, on_device(): lax.all_to_all(key_rows, 'head', split_axis=1, concat_axis=0, tiled=True)  7.13 us
  transfers between devices with their start and end apart: 8, of which 5 were waited for; matrix products, arithmetic and copies ran while one was open for 6% of the time, Pallas kernels for 0%

profile of v1, /device:TPU:0, one launch (start us, length us, event | category | flops | bytes accessed | tf_op | source)
XLA Modules:
  0.0 319.2 jit_solution(2125154517383322702)
XLA Ops:
  1.6 2.5 collective-permute-start
  4.8 1.9 copy.37
  6.7 3.5 %all-to-all-start.1 = ((bf16[96,4,768]{2,0,1:T(8,128)(2,1)}), bf16[96,4,768]{2,0,1:T(8,128)(2,1)S(1)}, u32[]{:S(2)}, u32[]{:S(2)}) async-start(bf16[96,4,768]{2,0,1:T(8,128)(2,1)} %bitcast.52), calls=%async_computation.1 | async-start | bytes 1179648 | tf_op jit(solution)/shard_map/all_to_all | solution.py:34
  10.3 2.0 collective-permute-done.1
  12.6 7.1 %all-to-all-done.1 = bf16[96,4,768]{2,0,1:T(8,128)(2,1)S(1)} async-done(((bf16[96,4,768]{2,0,1:T(8,128)(2,1)}), bf16[96,4,768]{2,0,1:T(8,128)(2,1)S(1)}, u32[]{:S(2)}, u32[]{:S(2)}) %all-to-all-start.1) | async-done | bytes 589856 | tf_op jit(solution)/shard_map/all_to_all | solution.py:34
  19.9 1.6 collective-permute-start.3
  21.5 2.2 collective-permute-start.4
  23.7 26.9 %collective-permute-done.3 = bf16[2,1,384,768]{3,2,0,1:T(8,128)(2,1)S(1)} collective-permute-done((bf16[2,1,384,768]{3,2,0,1:T(8,128)(2,1)S(1)}, bf16[2,1,384,768]{3,2,0,1:T(8,128)(2,1)S(1)}, u32[]{:S(2)}, u32[]{:S(2)}) %collective-permute-start.3) | collective-permute-done | bytes 1179680 | tf_op jit(solution)/shard_map/ppermute | solution.py:25
  50.6 23.3 %collective-permute-done.4 = bf16[2,1,384,768]{3,2,0,1:T(8,128)(2,1)S(1)} collective-permute-done((bf16[2,1,384,768]{3,2,0,1:T(8,128)(2,1)S(1)}, bf16[2,1,384,768]{3,2,0,1:T(8,128)(2,1)S(1)}, u32[]{:S(2)}, u32[]{:S(2)}) %collective-permute-start.4) | collective-permute-done | bytes 1179680 | tf_op jit(solution)/shard_map/ppermute | solution.py:25
  73.9 2.0 fusion.32
  78.1 4.2 %all-to-all-start = ((bf16[96,4,768]{2,0,1:T(8,128)(2,1)}), bf16[96,4,768]{2,0,1:T(8,128)(2,1)}, u32[]{:S(2)}, u32[]{:S(2)}) async-start(bf16[96,4,768]{2,0,1:T(8,128)(2,1)} %bitcast.77), calls=%async_computation | async-start | bytes 1179648 | tf_op jit(solution)/shard_map/all_to_all | solution.py:33
  82.4 148.5 %collective-permute-done.5 = bf16[3,2,1,384,768]{4,3,1,0,2:T(8,128)(2,1)} collective-permute-done((bf16[3,2,1,384,768]{4,3,1,0,2:T(8,128)(2,1)}, bf16[3,2,1,384,768]{4,3,1,0,2:T(8,128)(2,1)}, u32[]{:S(2)}, u32[]{:S(2)}) %collective-permute-start.5) | collective-permute-done | bytes 3538976 | tf_op jit(solution)/shard_map/ppermute | solution.py:25
  230.8 8.4 %pad_maximum_fusion = bf16[3,3,2,1,384,768]{5,4,2,1,3,0:T(8,128)(2,1)} fusion(bf16[1,3,2,1,384,768]{5,4,2,1,3,0:T(8,128)(2,1)} %bitcast.10, bf16[1,3,2,1,384,768]{5,4,2,1,3,0:T(8,128)(2,1)S(1)} %get-tuple-element.112), kind=kLoop, calls=%fused_computation.36 | loop fusion | flops 10616832 | bytes 17694720 | tf_op jit(solution)/shard_map/stack | solution.py:47
  239.3 8.9 %fusion.37 = (bf16[3,3,1,1,384,768]{5,4,2,1,3,0:T(8,128)(2,1)}, bf16[3,3,1,1,384,768]{5,4,2,1,3,0:T(8,128)(2,1)}) fusion(bf16[3,3,2,1,384,768]{5,4,2,1,3,0:T(8,128)(2,1)} %pad_maximum_fusion), kind=kLoop, calls=%fused_computation.59 | loop fusion | bytes 21233664 | tf_op jit(solution)/shard_map/slice | solution.py:49
  248.2 56.1 %while.12 = (s32[]{:T(128)}, bf16[6,1,384,128]{3,2,1,0:T(8,128)(2,1)}, s32[6]{0:T(128)S(1)}, bf16[384,768]{1,0:T(8,128)(2,1)}, bf16[9,384,768]{2,1,0:T(8,128)(2,...) while((s32[]{:T(128)}, ...), condition=%wide.region_3.5_spmd.clone.clone, body=%wide.region_0.4_spmd.clone.clone.sunk | while | flops 692404736 | bytes 28541528 | solution.py:87
  249.5 1.6 constant_dynamic-slice_fusion.3
  252.9 1.9 select_reduce_fusion.2
  255.9 1.6 fusion.52
  258.9 1.6 constant_dynamic-slice_fusion.3
  262.3 1.9 select_reduce_fusion.2
  265.2 1.6 fusion.52
  268.2 1.6 constant_dynamic-slice_fusion.3
  271.6 1.9 select_reduce_fusion.2
  274.6 1.6 fusion.52
  277.6 1.6 constant_dynamic-slice_fusion.3
  281.0 1.9 select_reduce_fusion.2
  283.9 1.6 fusion.52
  290.3 1.9 select_reduce_fusion.2
  293.3 1.6 fusion.52
  299.6 1.9 select_reduce_fusion.2
  302.6 1.6 fusion.52
  306.4 11.9 %all_to_all.54 = bf16[4,96,768]{2,1,0:T(8,128)(2,1)S(1)} all-to-all(bf16[4,96,768]{2,1,0:T(8,128)(2,1)S(1)} %all_to_all.47), channel_id=1, replica_groups=mesh['groups'=2,'ctx'=4,'head'=4] {'head'}, dimensions={0} | all-to-all | bytes 1179648 | tf_op jit(solution)/shard_map/all_to_all | solution.py:89
  (92 shorter events, 32.3 us)
Async XLA Ops:
  1.6 8.7 %collective-permute-start = (bf16[96,768]{1,0:T(8,128)(2,1)S(1)}, bf16[96,768]{1,0:T(8,128)(2,1)S(1)}, u32[]{:S(2)}, u32[]{:S(2)}) collective-permute-start(bf16[96,768]{1,0:T(8,128)(2,1)S(1)} %get-tuple-element.118), channel_id=1, source_target_pairs={{0,3},{1,0},{2,1},{3,2},{4,7},{5,4},{6,5},{7,6},{8,11},{9,8},{10,9... | collective-permute-start | bytes 442376 | tf_op jit(solution)/shard_map/ppermute | solution.py:17
  4.1 8.2 %collective-permute-start.1 = (bf16[96,768]{1,0:T(8,128)(2,1)S(1)}, bf16[96,768]{1,0:T(8,128)(2,1)S(1)}, u32[]{:S(2)}, u32[]{:S(2)}) collective-permute-start(bf16[96,768]{1,0:T(8,128)(2,1)S(1)} %get-tuple-element.117), channel_id=1, source_target_pairs={{0,2},{1,3},{2,0},{3,1},{4,6},{5,7},{6,4},{7,5},{8,10},{9,11},{10,... | collective-permute-start | bytes 442376 | tf_op jit(solution)/shard_map/ppermute | solution.py:17
  4.7 7.6 %collective-permute-start.2 = (bf16[96,768]{1,0:T(8,128)(2,1)S(1)}, bf16[96,768]{1,0:T(8,128)(2,1)S(1)}, u32[]{:S(2)}, u32[]{:S(2)}) collective-permute-start(bf16[96,768]{1,0:T(8,128)(2,1)S(1)} %get-tuple-element.116), channel_id=1, source_target_pairs={{0,1},{1,2},{2,3},{3,0},{4,5},{5,6},{6,7},{7,4},{8,9},{9,10},{10,1... | collective-permute-start | bytes 442376 | tf_op jit(solution)/shard_map/ppermute | solution.py:17
  6.7 13.0 %all-to-all-start.1 = ((bf16[96,4,768]{2,0,1:T(8,128)(2,1)}), bf16[96,4,768]{2,0,1:T(8,128)(2,1)S(1)}, u32[]{:S(2)}, u32[]{:S(2)}) async-start(bf16[96,4,768]{2,0,1:T(8,128)(2,1)} %bitcast.52), calls=%async_computation.1 | async-start | bytes 1179648 | tf_op jit(solution)/shard_map/all_to_all | solution.py:34
  19.9 30.7 %collective-permute-start.3 = (bf16[2,1,384,768]{3,2,0,1:T(8,128)(2,1)S(1)}, bf16[2,1,384,768]{3,2,0,1:T(8,128)(2,1)S(1)}, u32[]{:S(2)}, u32[]{:S(2)}) collective-permute-start(bf16[2,1,384,768]{3,2,0,1:T(8,128)(2,1)S(1)} %get-tuple-element.115), channel_id=1, source_target_pairs={{12,0},{0,4},{4,8},{8,12},{13,1},{1,5},{5,9},{9,13},{14,2},{2,6},{... | collective-permute-start | bytes 3538952 | tf_op jit(solution)/shard_map/ppermute | solution.py:25
  21.5 52.4 %collective-permute-start.4 = (bf16[2,1,384,768]{3,2,0,1:T(8,128)(2,1)S(1)}, bf16[2,1,384,768]{3,2,0,1:T(8,128)(2,1)S(1)}, u32[]{:S(2)}, u32[]{:S(2)}) collective-permute-start(bf16[2,1,384,768]{3,2,0,1:T(8,128)(2,1)S(1)} %get-tuple-element.115), channel_id=1, source_target_pairs={{4,0},{8,4},{12,8},{0,12},{5,1},{9,5},{13,9},{1,13},{6,2},{10,6},{... | collective-permute-start | bytes 3538952 | tf_op jit(solution)/shard_map/ppermute | solution.py:25
  73.9 3.3 %copy-start = (bf16[96,3072]{1,0:T(8,128)(2,1)S(1)}, bf16[96,3072]{1,0:T(8,128)(2,1)}, u32[]{:S(2)}) copy-start(bf16[96,3072]{1,0:T(8,128)(2,1)} %param.8) | copy-start | bytes 1769476
  73.9 8.4 %copy-start.1 = (s32[1,27]{1,0:T(1,128)S(1)}, s32[1,27]{1,0:T(1,128)}, u32[]{:S(2)}) copy-start(s32[1,27]{1,0:T(1,128)} %param.11) | copy-start | bytes 328
  75.9 154.9 %collective-permute-start.5 = (bf16[3,2,1,384,768]{4,3,1,0,2:T(8,128)(2,1)}, bf16[3,2,1,384,768]{4,3,1,0,2:T(8,128)(2,1)}, u32[]{:S(2)}, u32[]{:S(2)}) collective-permute-start(bf16[3,2,1,384,768]{4,3,1,0,2:T(8,128)(2,1)} %get-tuple-element.113), channel_id=1, source_target_pairs={{8,0},{12,4},{0,8},{4,12},{9,1},{13,5},{1,9},{5,13},{10,2},{14,6},... | collective-permute-start | bytes 10616840 | tf_op jit(solution)/shard_map/ppermute | solution.py:25
  78.1 170.1 %all-to-all-start = ((bf16[96,4,768]{2,0,1:T(8,128)(2,1)}), bf16[96,4,768]{2,0,1:T(8,128)(2,1)}, u32[]{:S(2)}, u32[]{:S(2)}) async-start(bf16[96,4,768]{2,0,1:T(8,128)(2,1)} %bitcast.77), calls=%async_computation | async-start | bytes 1179648 | tf_op jit(solution)/shard_map/all_to_all | solution.py:33
